TPU v7x, 32 devices: a whole 2x2x4 slice. The times are simulated.
32 devices in a mesh: lat: 8 (over z, y), lay: 4 (over x, core).
Axes of the slice: x: 2, y: 2, z: 4, core: 2. Of those that a mesh axis runs over, the one named last changes fastest.
Arguments:
- wave_field: float32 [2, 32, 512, 512], P(None, 'lay', 'lat'), may hold values from -6 to 6
- contrast: float32 [32, 512, 512], P('lay', 'lat'), may hold values from 0.1 to 1.5
- layer_of_plane: int32 [32], replicated, may hold values from 0 to 7, never falling along the last dimension, each value on 1 to 8 neighbouring positions
- toeplitz_table: float32 [2, 8, 63], replicated, may hold values from -1 to 1
- hankel_table: float32 [2, 8, 63], replicated, may hold values from -1 to 1
- layer_rates: float32 [8], replicated, may hold values from 0.5 to 1.5
Outputs:
- scattered_field: float32 [2, 32, 512, 512], P(None, 'lay', 'lat')
Inputs may be any that keep to these rules, and one draw needn't show every extreme that they name: `layer_of_plane`: layer numbers never fall from one plane to the next; every layer holds 1 to 8 planes.
All inputs are finite; a program needn't handle non-finite values.
Results may differ from a plain program's by a relative error of at most 0.00007.
Values sent between devices are 32-bit elements; how exact they have to be, the bound alone decides.
A program may use at most 128 MiB of HBM per device.

v0:
```python
import math
import jax
import jax.numpy as jnp
from jax import lax
from jax.sharding import PartitionSpec as P

HIGHEST = lax.Precision.HIGHEST


def signed_of(index, amount):
    return jnp.where(index >= amount // 2, index - amount, index).astype(jnp.float32) / (amount / 2)


def phase_tables(rows, cols, amount, sign):
    index_row = lax.broadcasted_iota(jnp.int32, (rows, cols), 0)
    index_col = lax.broadcasted_iota(jnp.int32, (rows, cols), 1)
    angle = 2.0 * math.pi / amount * (index_row * index_col % amount).astype(jnp.float32)
    return (jnp.cos(angle), sign * jnp.sin(angle))


def complex_apply(real_part, imag_part, cos_table, sin_table, form):
    out_real = jnp.einsum(form, real_part, cos_table, precision=HIGHEST) - jnp.einsum(
        form, imag_part, sin_table, precision=HIGHEST
    )
    out_imag = jnp.einsum(form, real_part, sin_table, precision=HIGHEST) + jnp.einsum(
        form, imag_part, cos_table, precision=HIGHEST
    )
    return (out_real, out_imag)


def fourier_last(real_part, imag_part, sign, factor):
    amount = real_part.shape[-1]
    leading = real_part.shape[:-1]
    first = 1
    for divisor in range(1, math.isqrt(amount) + 1):
        if amount % divisor == 0:
            first = divisor
    second = amount // first
    flat_real = real_part.reshape(-1, second, first)
    flat_imag = imag_part.reshape(-1, second, first)
    cos_second, sin_second = phase_tables(second, second, second, sign)
    section_real, section_imag = complex_apply(
        flat_real, flat_imag, cos_second, sin_second, "pmn,mk->pkn"
    )
    twist_cos, twist_sin = phase_tables(second, first, amount, sign)
    turned_real = section_real * twist_cos - section_imag * twist_sin
    turned_imag = section_real * twist_sin + section_imag * twist_cos
    cos_first, sin_first = phase_tables(first, first, first, sign)
    final_real, final_imag = complex_apply(
        turned_real, turned_imag, cos_first, sin_first, "pkn,nj->pjk"
    )
    final_real = final_real.reshape(leading + (amount,)) * factor
    final_imag = final_imag.reshape(leading + (amount,)) * factor
    return (final_real, final_imag)


def pick_amplitudes(rows, index, width):
    positions = jnp.arange(width, dtype=jnp.int32)
    onehot = (index[:, :, None] == positions[None, None, :]).astype(jnp.float32)
    return jnp.einsum("pan,ain->pai", rows, onehot, precision=HIGHEST)


def body(wave_field, contrast, layer_of_plane, toeplitz_table, hankel_table, layer_rates):
    row_count = wave_field.shape[2]
    width_y = wave_field.shape[3]
    lat_count = lax.axis_size("lat")
    lay_count = lax.axis_size("lay")
    width_x = row_count * lat_count
    ky_band = width_y // lat_count
    table_width = toeplitz_table.shape[-1]
    plane_total = (table_width + 1) // 2
    layer_count = layer_rates.shape[0]
    spec_real, spec_imag = fourier_last(wave_field[0], wave_field[1], -1.0, 1.0)
    along_y = jnp.stack([spec_real, spec_imag], 2)
    freq_x = signed_of(jnp.arange(width_x, dtype=jnp.int32), width_x)
    ky_first = lax.axis_index("lat") * ky_band
    layer_ids = jnp.arange(layer_count, dtype=jnp.int32)

    def couple(z_out, z_in, source, ky_rows):
        onehot = (layer_of_plane[z_out][:, None] == layer_ids[None, :]).astype(jnp.float32)
        rate_out = jnp.dot(onehot, layer_rates, precision=HIGHEST)
        rows_toeplitz = jnp.einsum("al,pln->pan", onehot, toeplitz_table, precision=HIGHEST)
        rows_hankel = jnp.einsum("al,pln->pan", onehot, hankel_table, precision=HIGHEST)
        offset = z_out[:, None] - z_in[None, :]
        plane_sum = z_out[:, None] + z_in[None, :]
        amp_toeplitz = pick_amplitudes(rows_toeplitz, offset + plane_total - 1, table_width)
        amp_hankel = pick_amplitudes(rows_hankel, plane_sum, table_width)
        freq_y = signed_of(ky_rows, width_y)
        steepness = jnp.sqrt(1.0 + freq_y[:, None] ** 2 + freq_x[None, :] ** 2)
        scaled = rate_out[:, None, None, None] * steepness[None, None] / plane_total
        decay_toeplitz = jnp.exp(-scaled * jnp.abs(offset).astype(jnp.float32)[:, :, None, None])
        decay_hankel = jnp.exp(-scaled * (0.5 * plane_sum.astype(jnp.float32))[:, :, None, None])
        kern_real = (
            amp_toeplitz[0][:, :, None, None] * decay_toeplitz
            + amp_hankel[0][:, :, None, None] * decay_hankel
        )
        kern_imag = (
            amp_toeplitz[1][:, :, None, None] * decay_toeplitz
            + amp_hankel[1][:, :, None, None] * decay_hankel
        )
        real_src = source[None, :, 0]
        imag_src = source[None, :, 1]
        out_real = jnp.sum(kern_real * real_src - kern_imag * imag_src, axis=1)
        out_imag = jnp.sum(kern_real * imag_src + kern_imag * real_src, axis=1)
        return jnp.stack([out_real, out_imag], 1)

    narrow = ky_band // lay_count
    narrow_rows = ky_first + lax.axis_index("lay") * narrow + jnp.arange(narrow, dtype=jnp.int32)
    lines_in = lax.all_to_all(along_y, "lat", split_axis=3, concat_axis=1, tiled=True)
    line_real = jnp.transpose(lines_in[:, :, 0], (0, 2, 1))
    line_imag = jnp.transpose(lines_in[:, :, 1], (0, 2, 1))
    out_real, out_imag = fourier_last(line_real, line_imag, -1.0, 1.0)
    spectrum = jnp.stack([out_real, out_imag], 1)
    gathered = lax.all_to_all(spectrum, "lay", split_axis=2, concat_axis=0, tiled=True)
    all_planes = gathered.shape[0]
    every_plane = jnp.arange(all_planes, dtype=jnp.int32)
    block_size = math.gcd(all_planes, 8)

    def one_block(which):
        z_out = which * block_size + jnp.arange(block_size, dtype=jnp.int32)
        return couple(z_out, every_plane, gathered, narrow_rows)

    stacked = lax.map(one_block, jnp.arange(all_planes // block_size, dtype=jnp.int32))
    coupled = stacked.reshape(all_planes, 2, narrow_rows.shape[0], width_x)
    mixed = lax.all_to_all(coupled, "lay", split_axis=0, concat_axis=2, tiled=True)
    out_real, out_imag = fourier_last(mixed[:, 0], mixed[:, 1], 1.0, 1.0 / width_x)
    spatial_x = jnp.transpose(jnp.stack([out_real, out_imag], 1), (0, 3, 1, 2))
    lines = lax.all_to_all(spatial_x, "lat", split_axis=1, concat_axis=3, tiled=True)
    space_real, space_imag = fourier_last(lines[:, :, 0], lines[:, :, 1], 1.0, 1.0 / width_y)
    return jnp.stack([space_real, space_imag], 0) * contrast[None]


def solution(mesh):
    return jax.shard_map(
        body,
        mesh=mesh,
        in_specs=(P(None, "lay", "lat", None), P("lay", "lat", None), P(), P(), P(), P()),
        out_specs=P(None, "lay", "lat", None),
        check_vma=False,
    )
```

profile of v0, /device:TPU:0, one launch (start us, length us, event | category | flops | bytes accessed | tf_op | source)
XLA Modules:
  0.0 411.3 jit_solution(14716647917819366938)
XLA Ops:
  0.1 2.8 fusion.334
  24.7 2.7 fusion.40
  29.8 3.8 copy_bitcast_fusion.3
  33.6 5.9 %reshape.337 = f32[8,1,65536]{2,1,0:T(1,128)S(1)} reshape(f32[512,2,8,64]{3,2,1,0:T(8,128)} %copy_bitcast_fusion.3) | data formatting | bytes 4194304
  39.6 55.8 %all_to_all.72 = f32[8,1,65536]{2,1,0:T(1,128)} all-to-all(f32[8,1,65536]{2,1,0:T(1,128)S(1)} %reshape.337), channel_id=1, replica_groups=mesh['lat'=8,'lay'=4] {'lat'}, dimensions={0} | all-to-all | bytes 4194304 | tf_op jit(solution)/shard_map/all_to_all | solution.py:109
  95.9 7.1 %reduce = f32[8,65536]{1,0:T(8,128)S(1)} reduce(f32[8,1,65536]{2,1,0:T(1,128)} %all_to_all.72, f32[]{:T(128)} %broadcast.832), dimensions={1}, to_apply=%all_to_all.52.reduce_sub_computation | reduce | bytes 4194308 | tf_op jit(solution)/shard_map/all_to_all | solution.py:109
  103.0 3.6 reshape.338
  106.6 6.6 %copy.340 = f32[8,64,2,8,64]{1,3,4,2,0:T(8,128)} copy(f32[8,64,2,8,64]{1,0,2,4,3:T(8,128)} %bitcast.274) | data formatting | bytes 4194304 | tf_op jit(solution)/shard_map/all_to_all | solution.py:109
  113.3 3.6 all_to_all.55
  141.6 2.7 fusion.38
  146.7 3.8 pad_maximum_fusion.1
  150.5 4.5 %copy.221 = f32[8,2,64,512]{3,0,1,2:T(8,128)} copy(f32[8,2,64,512]{2,0,3,1:T(8,128)} %pad_maximum_fusion.1) | data formatting | bytes 4194304 | tf_op jit(solution)/shard_map/stack | solution.py:113
  155.0 3.6 all-to-all-start.1
  158.6 25.6 %all-to-all-done.1 = f32[8,2,64,512]{3,0,1,2:T(8,128)S(1)} async-done(((f32[8,2,64,512]{3,0,1,2:T(8,128)}), f32[8,2,64,512]{3,0,1,2:T(8,128)S(1)}, u32[]{:S(2)}, u32[]{:S(2)}) %all-to-all-start.1) | async-done | bytes 2097184 | tf_op jit(solution)/shard_map/all_to_all | solution.py:114
  186.2 46.6 %while.16 = (s32[]{:T(128)}, f32[4,8,2,16,512]{4,3,2,1,0:T(8,128)}, s32[4]{0:T(128)S(1)}, s32[32]{0:T(128)S(1)}, f32[2,8,63]{2,1,0:T(8,128)S(1)}, /*index=5*/f32...) while((s32[]{:T(128)}, f32[4,8,2,16,512]{4,3,2,1,0:T(8,128)}, ...), condition=%wide.region_3.4_spmd.clone.clone, body=%wide.region_0.3_spmd.clone.clone.sunk | while | flops 34766440 | bytes 8512337 | solution.py:123
  190.0 7.1 %subtract_reduce_fusion.2 = (f32[8,16,512]{2,1,0:T(8,128)S(1)}, f32[8,16,512]{2,1,0:T(8,128)S(1)}) fusion(f32[32,16,512]{2,1,0:T(8,128)S(1)} %get-tuple-element.422, f32[8,32]{1,0:T(8,128)S(1)} %bitcast.286, f32[8,32]{1,0:T(8,128)S(1)} %bitcast.288, f32[32,16,512]{2,1,0:T(8,128)S(1)} %get-tuple-element.427, f32[8,32]{1,0:T(8,128)S(1)} %convert_multiply_fusion.2, ...), kind=kLoop, calls=%fused_computation.6.clone.1 | loop fusion | flops 33423360 | bytes 2889728 | tf_op jit(solution)/shard_map/while/body/eval_jaxpr/reduce_sum | solution.py:103
  201.6 7.1 %subtract_reduce_fusion.2 = (f32[8,16,512]{2,1,0:T(8,128)S(1)}, f32[8,16,512]{2,1,0:T(8,128)S(1)}) fusion(f32[32,16,512]{2,1,0:T(8,128)S(1)} %get-tuple-element.422, f32[8,32]{1,0:T(8,128)S(1)} %bitcast.286, f32[8,32]{1,0:T(8,128)S(1)} %bitcast.288, f32[32,16,512]{2,1,0:T(8,128)S(1)} %get-tuple-element.427, f32[8,32]{1,0:T(8,128)S(1)} %convert_multiply_fusion.2, ...), kind=kLoop, calls=%fused_computation.6.clone.1 | loop fusion | flops 33423360 | bytes 2889728 | tf_op jit(solution)/shard_map/while/body/eval_jaxpr/reduce_sum | solution.py:103
  213.3 7.1 %subtract_reduce_fusion.2 = (f32[8,16,512]{2,1,0:T(8,128)S(1)}, f32[8,16,512]{2,1,0:T(8,128)S(1)}) fusion(f32[32,16,512]{2,1,0:T(8,128)S(1)} %get-tuple-element.422, f32[8,32]{1,0:T(8,128)S(1)} %bitcast.286, f32[8,32]{1,0:T(8,128)S(1)} %bitcast.288, f32[32,16,512]{2,1,0:T(8,128)S(1)} %get-tuple-element.427, f32[8,32]{1,0:T(8,128)S(1)} %convert_multiply_fusion.2, ...), kind=kLoop, calls=%fused_computation.6.clone.1 | loop fusion | flops 33423360 | bytes 2889728 | tf_op jit(solution)/shard_map/while/body/eval_jaxpr/reduce_sum | solution.py:103
  224.9 7.1 %subtract_reduce_fusion.2 = (f32[8,16,512]{2,1,0:T(8,128)S(1)}, f32[8,16,512]{2,1,0:T(8,128)S(1)}) fusion(f32[32,16,512]{2,1,0:T(8,128)S(1)} %get-tuple-element.422, f32[8,32]{1,0:T(8,128)S(1)} %bitcast.286, f32[8,32]{1,0:T(8,128)S(1)} %bitcast.288, f32[32,16,512]{2,1,0:T(8,128)S(1)} %get-tuple-element.427, f32[8,32]{1,0:T(8,128)S(1)} %convert_multiply_fusion.2, ...), kind=kLoop, calls=%fused_computation.6.clone.1 | loop fusion | flops 33423360 | bytes 2889728 | tf_op jit(solution)/shard_map/while/body/eval_jaxpr/reduce_sum | solution.py:103
  232.9 4.0 all-to-all-start.2
  236.9 25.6 %all-to-all-done.2 = f32[32,2,16,512]{3,2,1,0:T(8,128)S(1)} async-done(((f32[32,2,16,512]{3,2,1,0:T(8,128)}), f32[32,2,16,512]{3,2,1,0:T(8,128)S(1)}, u32[]{:S(2)}, u32[]{:S(2)}) %all-to-all-start.2) | async-done | bytes 2097184 | tf_op jit(solution)/shard_map/all_to_all | solution.py:125
  285.7 2.7 fusion.35
  290.8 3.8 copy_bitcast_fusion.2
  294.6 7.2 %reshape.339 = f32[8,1,65536]{2,1,0:T(1,128)} reshape(f32[512,2,8,64]{3,2,1,0:T(8,128)} %copy_bitcast_fusion.2) | data formatting | bytes 4194304
  301.9 4.9 %all-to-all-start.3 = ((f32[8,1,65536]{2,1,0:T(1,128)}), f32[8,1,65536]{2,1,0:T(1,128)}, u32[]{:S(2)}, u32[]{:S(2)}) async-start(f32[8,1,65536]{2,1,0:T(1,128)} %reshape.339), calls=%async_computation.3 | async-start | bytes 4194304 | tf_op jit(solution)/shard_map/all_to_all | solution.py:128
  308.8 46.2 %all-to-all-done.3 = f32[8,1,65536]{2,1,0:T(1,128)} async-done(((f32[8,1,65536]{2,1,0:T(1,128)}), f32[8,1,65536]{2,1,0:T(1,128)}, u32[]{:S(2)}, u32[]{:S(2)}) %all-to-all-start.3) | async-done | bytes 2097184 | tf_op jit(solution)/shard_map/all_to_all | solution.py:128
  354.9 7.1 %reduce.1 = f32[8,65536]{1,0:T(8,128)S(1)} reduce(f32[8,1,65536]{2,1,0:T(1,128)} %all-to-all-done.3, f32[]{:T(128)} %broadcast.832), dimensions={1}, to_apply=%all_to_all.64.reduce_sub_computation | reduce | bytes 4194308 | tf_op jit(solution)/shard_map/all_to_all | solution.py:128
  362.1 3.6 reshape.340
  365.7 6.6 %copy.339 = f32[8,8,64,2,64]{4,1,2,3,0:T(8,128)} copy(f32[8,8,64,2,64]{4,0,3,2,1:T(8,128)} %bitcast.276) | data formatting | bytes 4194304 | tf_op jit(solution)/shard_map/all_to_all | solution.py:128
  372.3 3.6 all_to_all.67
  402.8 4.5 %maximum_multiply_fusion = f32[2,8,64,512]{2,1,3,0:T(8,128)} fusion(f32[1,8,64,512]{2,1,3,0:T(8,128)} %mul.831, f32[1,8,64,512]{2,1,3,0:T(8,128)} %mul.828, f32[8,64,512]{1,0,2:T(8,128)S(1)} %copy-done.1), kind=kLoop, calls=%fused_computation.56 | loop fusion | flops 1048576 | bytes 5242880 | tf_op jit(solution)/shard_map/mul | solution.py:130
  407.4 3.8 copy.254
  (181 shorter events, 123.3 us)
Async XLA Ops:
  4.1 4.2 %copy-start.9 = (f32[1,8,64,512]{3,2,1,0:T(8,128)S(1)}, f32[1,8,64,512]{3,2,1,0:T(8,128)}, u32[]{:S(2)}) copy-start(f32[1,8,64,512]{3,2,1,0:T(8,128)} %get-tuple-element.352) | copy-start | bytes 3145732
  10.3 2.2 copy-start.2
  121.0 4.2 %copy-start.6 = (f32[8,64,512]{2,1,0:T(8,128)S(1)}, f32[8,64,512]{2,1,0:T(8,128)}, u32[]{:S(2)}) copy-start(f32[8,64,512]{2,1,0:T(8,128)} %get-tuple-element.350) | copy-start | bytes 3145732
  127.2 2.0 copy-start.3
  155.0 29.2 %all-to-all-start.1 = ((f32[8,2,64,512]{3,0,1,2:T(8,128)}), f32[8,2,64,512]{3,0,1,2:T(8,128)S(1)}, u32[]{:S(2)}, u32[]{:S(2)}) async-start(f32[8,2,64,512]{3,0,1,2:T(8,128)} %copy.221), calls=%async_computation.1 | async-start | bytes 4194304 | tf_op jit(solution)/shard_map/all_to_all | solution.py:114
  185.5 0.7 copy-start
  185.5 0.7 copy-start.11
  185.5 0.7 copy-start.12
  185.5 0.7 copy-start.13
  232.9 29.6 %all-to-all-start.2 = ((f32[32,2,16,512]{3,2,1,0:T(8,128)}), f32[32,2,16,512]{3,2,1,0:T(8,128)S(1)}, u32[]{:S(2)}, u32[]{:S(2)}) async-start(f32[32,2,16,512]{3,2,1,0:T(8,128)} %bitcast.22), calls=%async_computation.2 | async-start | bytes 4194304 | tf_op jit(solution)/shard_map/all_to_all | solution.py:125
  265.1 4.2 %copy-start.7 = (f32[8,1,64,512]{3,2,1,0:T(8,128)S(1)}, f32[8,1,64,512]{3,2,1,0:T(8,128)}, u32[]{:S(2)}) copy-start(f32[8,1,64,512]{3,2,1,0:T(8,128)} %get-tuple-element.348) | copy-start | bytes 3145732
  271.3 2.2 copy-start.4
  301.9 4.9 %copy-start.10 = (f32[8,64,512]{2,1,0:T(8,128)S(1)}, f32[8,64,512]{2,1,0:T(8,128)}, u32[]{:S(2)}) copy-start(f32[8,64,512]{2,1,0:T(8,128)} %param.9) | copy-start | bytes 3145732
  301.9 53.1 %all-to-all-start.3 = ((f32[8,1,65536]{2,1,0:T(1,128)}), f32[8,1,65536]{2,1,0:T(1,128)}, u32[]{:S(2)}, u32[]{:S(2)}) async-start(f32[8,1,65536]{2,1,0:T(1,128)} %reshape.339), calls=%async_computation.3 | async-start | bytes 4194304 | tf_op jit(solution)/shard_map/all_to_all | solution.py:128
  380.0 4.2 %copy-start.8 = (f32[8,64,1,512]{3,1,2,0:T(8,128)S(1)}, f32[8,64,1,512]{3,1,2,0:T(8,128)}, u32[]{:S(2)}) copy-start(f32[8,64,1,512]{3,1,2,0:T(8,128)} %get-tuple-element.346) | copy-start | bytes 3145732
  386.2 2.0 copy-start.5
  400.8 2.0 copy-start.1
where the time goes:
time: 417 us; the launch traced here: 411 us
  local copies, waits for them, and re-layouts  113 us (27%)
  waiting for transfers between devices  97.3 us (23%)
  matrix products  65.9 us (16%)
  other arithmetic  63.4 us (15%)
  blocking collectives  55.8 us (13%)
  starting transfers between devices  12.5 us (3%)
    all_to_all x1, blocking collectives, body(): lax.all_to_all(along_y, 'lat', split_axis=3, concat_axis=1, tiled=True)  55.8 us
    all_to_all x1, waiting for transfers between devices, body(): lax.all_to_all(spatial_x, 'lat', split_axis=1, concat_axis=3, tiled=True)  46.2 us
    reduce_sum x4, other arithmetic, couple(): out_real = jnp.sum(kern_real * real_src - kern_imag * imag_src, axis=1)  28.2 us
    all_to_all x1, waiting for transfers between devices, body(): lax.all_to_all(spectrum, 'lay', split_axis=2, concat_axis=0, tiled=True)  25.6 us
    all_to_all x1, waiting for transfers between devices, body(): lax.all_to_all(coupled, 'lay', split_axis=0, concat_axis=2, tiled=True)  25.6 us
    unnamed x34, local copies, waits for them, and re-layouts  23.4 us
    dot_general x8, matrix products, complex_apply(): jnp.einsum(form, real_part, sin_table, precision=HIGHEST)  19.4 us
    dot_general x8, matrix products, complex_apply(): jnp.einsum(form, imag_part, cos_table, precision=HIGHEST)  16.2 us
  transfers between devices with their start and end apart: 3, of which 3 were waited for; matrix products, arithmetic and copies ran while one was open for 1% of the time, Pallas kernels for 0%

commit v1 on v0

--- a/solution.py
+++ b/solution.py
@@ -111,7 +111,10 @@
     line_imag = jnp.transpose(lines_in[:, :, 1], (0, 2, 1))
     out_real, out_imag = fourier_last(line_real, line_imag, -1.0, 1.0)
     spectrum = jnp.stack([out_real, out_imag], 1)
-    gathered = lax.all_to_all(spectrum, "lay", split_axis=2, concat_axis=0, tiled=True)
+    gathered = jnp.concatenate(
+        lax.all_to_all(jnp.stack(jnp.split(spectrum, lax.axis_size("lay"), axis=2)), "lay", 0, 0),
+        axis=0,
+    )
     all_planes = gathered.shape[0]
     every_plane = jnp.arange(all_planes, dtype=jnp.int32)
     block_size = math.gcd(all_planes, 8)

time: 417 us -> 432 us (1.036)
  local copies, waits for them, and re-layouts: 113 us -> 130 us
    another operation x0 -> x5, local copies, waits for them, and re-layouts: none -> 18.6 us  [body(): jnp.stack(jnp.split(spectrum, lax.axis_size('lay'), axis=2))]
    another operation x3, local copies, waits for them, and re-layouts: 8.04 us -> 3.67 us  [body(): spectrum = jnp.stack([out_real, out_imag], 1)]
    unnamed x34 -> x37, local copies, waits for them, and re-layouts: 23.4 us -> 27.6 us
  transfers between devices with their start and end apart: 3 -> 3, of which waited for: 3 -> 3; matrix products, arithmetic and copies ran while one was open for 1% -> 0% of each run, Pallas kernels for 0% -> 0%
where the time goes in v1:
time: 432 us; the launch traced here: 427 us
  local copies, waits for them, and re-layouts  130 us (30%)
  waiting for transfers between devices  97.3 us (23%)
  matrix products  65.9 us (15%)
  other arithmetic  61.2 us (14%)
  blocking collectives  55.8 us (13%)
  starting transfers between devices  12.5 us (3%)
    all_to_all x1, blocking collectives, body(): lax.all_to_all(along_y, 'lat', split_axis=3, concat_axis=1, tiled=True)  55.8 us
    all_to_all x1, waiting for transfers between devices, body(): lax.all_to_all(spatial_x, 'lat', split_axis=1, concat_axis=3, tiled=True)  46.1 us
    reduce_sum x4, other arithmetic, couple(): out_real = jnp.sum(kern_real * real_src - kern_imag * imag_src, axis=1)  28.2 us
    unnamed x37, local copies, waits for them, and re-layouts  27.6 us
    all_to_all x1, waiting for transfers between devices, body(): lax.all_to_all(jnp.stack(jnp.split(spectrum, lax.axis_size('lay'), axis=2...  25.6 us
    all_to_all x1, waiting for transfers between devices, body(): lax.all_to_all(coupled, 'lay', split_axis=0, concat_axis=2, tiled=True)  25.6 us
    another operation x5, local copies, waits for them, and re-layouts, body(): jnp.stack(jnp.split(spectrum, lax.axis_size('lay'), axis=2))  18.6 us
    dot_general x8, matrix products, complex_apply(): jnp.einsum(form, real_part, sin_table, precision=HIGHEST)  18.4 us
  transfers between devices with their start and end apart: 3, of which 3 were waited for; matrix products, arithmetic and copies ran while one was open for 0% of the time, Pallas kernels for 0%

profile of v1, /device:TPU:0, one launch (start us, length us, event | category | flops | bytes accessed | tf_op | source)
XLA Modules:
  0.0 426.6 jit_solution(14146244545969589838)
XLA Ops:
  0.1 2.8 fusion.334
  29.8 3.8 copy_bitcast_fusion.3
  33.6 5.9 %reshape.341 = f32[8,1,65536]{2,1,0:T(1,128)S(1)} reshape(f32[512,2,8,64]{3,2,1,0:T(8,128)} %copy_bitcast_fusion.3) | data formatting | bytes 4194304
  39.6 55.8 %all_to_all.59 = f32[8,1,65536]{2,1,0:T(1,128)} all-to-all(f32[8,1,65536]{2,1,0:T(1,128)S(1)} %reshape.341), channel_id=1, replica_groups=mesh['lat'=8,'lay'=4] {'lat'}, dimensions={0} | all-to-all | bytes 4194304 | tf_op jit(solution)/shard_map/all_to_all | solution.py:109
  95.9 7.2 %reduce = f32[8,65536]{1,0:T(8,128)S(1)} reduce(f32[8,1,65536]{2,1,0:T(1,128)} %all_to_all.59, f32[]{:T(128)} %broadcast.832), dimensions={1}, to_apply=%all_to_all.42.reduce_sub_computation | reduce | bytes 4194308 | tf_op jit(solution)/shard_map/all_to_all | solution.py:109
  103.1 3.6 reshape.342
  106.7 6.6 %copy.339 = f32[8,64,2,8,64]{1,3,4,2,0:T(8,128)} copy(f32[8,64,2,8,64]{1,0,2,4,3:T(8,128)} %bitcast.279) | data formatting | bytes 4194304 | tf_op jit(solution)/shard_map/all_to_all | solution.py:109
  113.3 3.6 all_to_all.45
  148.7 7.5 %slice_bitcast_fusion.5 = (f32[1,8,2,16,512]{3,1,4,2,0:T(8,128)}, f32[1,8,2,16,512]{3,1,4,2,0:T(8,128)}, f32[1,8,2,16,512]{3,1,4,2,0:T(8,128)}, f32[1,8,2,16,512]{3,1,4,2,0:T(8,128)}) fusion(f32[8,2,64,512]{2,0,3,1:T(8,128)S(1)} %constant_dynamic-update-slice_fusion), kind=kLoop, calls=%fused_computation.56 | loop fusion | bytes 4194304 | tf_op jit(solution)/shard_map/stack | solution.py:115
  156.1 2.8 copy.220
  158.9 2.8 copy.221
  161.7 2.8 copy.222
  164.5 2.8 copy.223
  168.9 3.6 all-to-all-start.1
  172.5 25.6 %all-to-all-done.1 = f32[4,8,2,16,512]{4,3,2,1,0:T(8,128)S(1)} async-done(((f32[4,8,2,16,512]{4,3,2,1,0:T(8,128)}), f32[4,8,2,16,512]{4,3,2,1,0:T(8,128)S(1)}, u32[]{:S(2)}, u32[]{:S(2)}) %all-to-all-start.1) | async-done | bytes 2097184 | tf_op jit(solution)/shard_map/all_to_all | solution.py:115
  201.3 46.7 %while.16 = (s32[]{:T(128)}, f32[4,8,2,16,512]{4,3,2,1,0:T(8,128)}, s32[4]{0:T(128)S(1)}, s32[32]{0:T(128)S(1)}, f32[2,8,63]{2,1,0:T(8,128)S(1)}, /*index=5*/f32...) while((s32[]{:T(128)}, f32[4,8,2,16,512]{4,3,2,1,0:T(8,128)}, ...), condition=%wide.region_3.4_spmd.clone.clone, body=%wide.region_0.3_spmd.clone.clone.sunk | while | flops 34766440 | bytes 8512337 | solution.py:126
  205.1 7.1 %subtract_reduce_fusion.2 = (f32[8,16,512]{2,1,0:T(8,128)S(1)}, f32[8,16,512]{2,1,0:T(8,128)S(1)}) fusion(f32[32,16,512]{2,1,0:T(8,128)S(1)} %get-tuple-element.426, f32[8,32]{1,0:T(8,128)S(1)} %bitcast.290, f32[8,32]{1,0:T(8,128)S(1)} %bitcast.292, f32[32,16,512]{2,1,0:T(8,128)S(1)} %get-tuple-element.431, f32[8,32]{1,0:T(8,128)S(1)} %convert_multiply_fusion.2, ...), kind=kLoop, calls=%fused_computation.6.clone.1 | loop fusion | flops 33423360 | bytes 2889728 | tf_op jit(solution)/shard_map/while/body/eval_jaxpr/reduce_sum | solution.py:103
  216.8 7.1 %subtract_reduce_fusion.2 = (f32[8,16,512]{2,1,0:T(8,128)S(1)}, f32[8,16,512]{2,1,0:T(8,128)S(1)}) fusion(f32[32,16,512]{2,1,0:T(8,128)S(1)} %get-tuple-element.426, f32[8,32]{1,0:T(8,128)S(1)} %bitcast.290, f32[8,32]{1,0:T(8,128)S(1)} %bitcast.292, f32[32,16,512]{2,1,0:T(8,128)S(1)} %get-tuple-element.431, f32[8,32]{1,0:T(8,128)S(1)} %convert_multiply_fusion.2, ...), kind=kLoop, calls=%fused_computation.6.clone.1 | loop fusion | flops 33423360 | bytes 2889728 | tf_op jit(solution)/shard_map/while/body/eval_jaxpr/reduce_sum | solution.py:103
  228.4 7.1 %subtract_reduce_fusion.2 = (f32[8,16,512]{2,1,0:T(8,128)S(1)}, f32[8,16,512]{2,1,0:T(8,128)S(1)}) fusion(f32[32,16,512]{2,1,0:T(8,128)S(1)} %get-tuple-element.426, f32[8,32]{1,0:T(8,128)S(1)} %bitcast.290, f32[8,32]{1,0:T(8,128)S(1)} %bitcast.292, f32[32,16,512]{2,1,0:T(8,128)S(1)} %get-tuple-element.431, f32[8,32]{1,0:T(8,128)S(1)} %convert_multiply_fusion.2, ...), kind=kLoop, calls=%fused_computation.6.clone.1 | loop fusion | flops 33423360 | bytes 2889728 | tf_op jit(solution)/shard_map/while/body/eval_jaxpr/reduce_sum | solution.py:103
  240.1 7.1 %subtract_reduce_fusion.2 = (f32[8,16,512]{2,1,0:T(8,128)S(1)}, f32[8,16,512]{2,1,0:T(8,128)S(1)}) fusion(f32[32,16,512]{2,1,0:T(8,128)S(1)} %get-tuple-element.426, f32[8,32]{1,0:T(8,128)S(1)} %bitcast.290, f32[8,32]{1,0:T(8,128)S(1)} %bitcast.292, f32[32,16,512]{2,1,0:T(8,128)S(1)} %get-tuple-element.431, f32[8,32]{1,0:T(8,128)S(1)} %convert_multiply_fusion.2, ...), kind=kLoop, calls=%fused_computation.6.clone.1 | loop fusion | flops 33423360 | bytes 2889728 | tf_op jit(solution)/shard_map/while/body/eval_jaxpr/reduce_sum | solution.py:103
  248.0 4.0 all-to-all-start.2
  252.1 25.6 %all-to-all-done.2 = f32[32,2,16,512]{3,2,1,0:T(8,128)S(1)} async-done(((f32[32,2,16,512]{3,2,1,0:T(8,128)}), f32[32,2,16,512]{3,2,1,0:T(8,128)S(1)}, u32[]{:S(2)}, u32[]{:S(2)}) %all-to-all-start.2) | async-done | bytes 2097184 | tf_op jit(solution)/shard_map/all_to_all | solution.py:128
  306.0 3.8 copy_bitcast_fusion.2
  309.8 7.2 %reshape.343 = f32[8,1,65536]{2,1,0:T(1,128)} reshape(f32[512,2,8,64]{3,2,1,0:T(8,128)} %copy_bitcast_fusion.2) | data formatting | bytes 4194304
  317.0 4.9 %all-to-all-start.3 = ((f32[8,1,65536]{2,1,0:T(1,128)}), f32[8,1,65536]{2,1,0:T(1,128)}, u32[]{:S(2)}, u32[]{:S(2)}) async-start(f32[8,1,65536]{2,1,0:T(1,128)} %reshape.343), calls=%async_computation.3 | async-start | bytes 4194304 | tf_op jit(solution)/shard_map/all_to_all | solution.py:131
  324.0 46.1 %all-to-all-done.3 = f32[8,1,65536]{2,1,0:T(1,128)} async-done(((f32[8,1,65536]{2,1,0:T(1,128)}), f32[8,1,65536]{2,1,0:T(1,128)}, u32[]{:S(2)}, u32[]{:S(2)}) %all-to-all-start.3) | async-done | bytes 2097184 | tf_op jit(solution)/shard_map/all_to_all | solution.py:131
  370.1 7.2 %reduce.1 = f32[8,65536]{1,0:T(8,128)S(1)} reduce(f32[8,1,65536]{2,1,0:T(1,128)} %all-to-all-done.3, f32[]{:T(128)} %broadcast.832), dimensions={1}, to_apply=%all_to_all.51.reduce_sub_computation | reduce | bytes 4194308 | tf_op jit(solution)/shard_map/all_to_all | solution.py:131
  377.3 3.6 reshape.344
  380.9 6.6 %copy.338 = f32[8,8,64,2,64]{4,1,2,3,0:T(8,128)} copy(f32[8,8,64,2,64]{4,0,3,2,1:T(8,128)} %bitcast.281) | data formatting | bytes 4194304 | tf_op jit(solution)/shard_map/all_to_all | solution.py:131
  387.5 3.6 all_to_all.54
  418.1 4.5 %maximum_multiply_fusion = f32[2,8,64,512]{2,1,3,0:T(8,128)} fusion(f32[1,8,64,512]{2,1,3,0:T(8,128)} %mul.831, f32[1,8,64,512]{2,1,3,0:T(8,128)} %mul.828, f32[8,64,512]{1,0,2:T(8,128)S(1)} %copy-done.1), kind=kLoop, calls=%fused_computation.59 | loop fusion | flops 1048576 | bytes 5242880 | tf_op jit(solution)/shard_map/mul | solution.py:133
  422.6 3.8 copy.254
  (188 shorter events, 136.3 us)
Async XLA Ops:
  4.1 4.2 copy-start.10
  10.3 2.2 copy-start.3
  121.1 4.2 copy-start.7
  127.2 2.0 copy-start.4
  168.9 29.2 %all-to-all-start.1 = ((f32[4,8,2,16,512]{4,3,2,1,0:T(8,128)}), f32[4,8,2,16,512]{4,3,2,1,0:T(8,128)S(1)}, u32[]{:S(2)}, u32[]{:S(2)}) async-start(f32[4,8,2,16,512]{4,3,2,1,0:T(8,128)} %pad_maximum_fusion.1), calls=%async_computation.1 | async-start | bytes 4194304 | tf_op jit(solution)/shard_map/all_to_all | solution.py:115
  198.1 1.3 copy-start.2
  199.4 1.9 copy-start
  199.4 1.9 copy-start.12
  199.4 1.9 copy-start.13
  199.4 1.9 copy-start.14
  248.0 29.6 %all-to-all-start.2 = ((f32[32,2,16,512]{3,2,1,0:T(8,128)}), f32[32,2,16,512]{3,2,1,0:T(8,128)S(1)}, u32[]{:S(2)}, u32[]{:S(2)}) async-start(f32[32,2,16,512]{3,2,1,0:T(8,128)} %bitcast.23), calls=%async_computation.2 | async-start | bytes 4194304 | tf_op jit(solution)/shard_map/all_to_all | solution.py:128
  280.3 4.2 copy-start.8
  286.4 2.2 copy-start.5
  317.0 4.9 %copy-start.11 = (f32[8,64,512]{2,1,0:T(8,128)S(1)}, f32[8,64,512]{2,1,0:T(8,128)}, u32[]{:S(2)}) copy-start(f32[8,64,512]{2,1,0:T(8,128)} %param.9) | copy-start | bytes 3145732
  317.0 53.1 %all-to-all-start.3 = ((f32[8,1,65536]{2,1,0:T(1,128)}), f32[8,1,65536]{2,1,0:T(1,128)}, u32[]{:S(2)}, u32[]{:S(2)}) async-start(f32[8,1,65536]{2,1,0:T(1,128)} %reshape.343), calls=%async_computation.3 | async-start | bytes 4194304 | tf_op jit(solution)/shard_map/all_to_all | solution.py:131
  395.2 4.2 copy-start.9
  401.4 2.0 copy-start.6
  416.0 2.0 copy-start.1
